TPU v7x, 32 devices: a whole 2x2x4 slice. The times are simulated.
32 devices in a mesh: dp: 8 (over z, y), own: 4 (over x, core).
Axes of the slice: x: 2, y: 2, z: 4, core: 2. Of those that a mesh axis runs over, the one named last changes fastest.
Arguments:
- acts_kv: bfloat16 [1024, 2560], P('dp', 'own'), may hold values from -6 to 6
- grads_kv: bfloat16 [1024, 1024], P('dp', 'own'), may hold values from -6 to 6
- acts_up: bfloat16 [1024, 2560], P('dp', 'own'), may hold values from -6 to 6
- grads_up: bfloat16 [1024, 3072], P('dp', 'own'), may hold values from -6 to 6
- prev_a_kv: float32 [4, 640, 640], P('own'), as said below
- prev_g_kv: float32 [4, 256, 256], P('own'), as said below
- prev_a_up: float32 [4, 640, 640], P('own'), as said below
- prev_g_up: float32 [4, 768, 768], P('own'), as said below
- owners: int32 [2, 4], replicated, may hold values from 0 to 7, as said below
- damping: float32 [4], replicated, may hold values from 0.05 to 0.5
- init_scale: float32 [4, 4], replicated, may hold values from 0.4 to 0.8
- weights_kv: float32 [2560, 1024], P('own', 'dp'), may hold values from -0.75 to 0.75
- weights_up: float32 [2560, 3072], P('own', 'dp'), may hold values from -0.75 to 0.75
- step_size: float32 [], replicated, may hold values from 0.2 to 0.5
Outputs:
- new_kv: float32 [2560, 1024], P('own', 'dp')
- new_up: float32 [2560, 3072], P('own', 'dp')
Inputs may be any that keep to these rules, and one draw needn't show every extreme that they name: `owners`: row 0 names for each factor the dp index that inverts it: one index is named by two factors, the others by one, and 0 and 7 are always named. Row 1 refreshes both factors of one of the two linears and leaves at least one factor of the other unrefreshed. `prev_a_kv`: every block is symmetric and positive definite. `prev_g_kv`: every block is symmetric and positive definite. `prev_a_up`: every block is symmetric and positive definite. `prev_g_up`: every block is symmetric and positive definite.
All inputs are finite; a program needn't handle non-finite values.
Results may differ from a plain program's by a relative error of at most 0.0021.
Values may be sent and summed in bfloat16 or wider, within the bound.
No kernel may reach another device: no remote copies, remote signals or barrier semaphores. Data moves between devices by JAX's collectives and lax.ppermute only.
A program may use at most 128 MiB of HBM per device.

v0:
```python
import jax
import jax.numpy as jnp
from jax import lax
from jax.sharding import PartitionSpec as P

D = 2560
OUT_KV = 1024
OUT_UP = 3072
NF = 4
NS_STEPS = 2


def spread(value, axis, root):
    mine = lax.axis_index(axis) == root
    return lax.psum(jnp.where(mine, value, jnp.zeros_like(value)), axis)


def matrix_product(left_side, right_side):
    return jnp.dot(
        left_side, right_side, preferred_element_type=jnp.float32, precision=lax.Precision.HIGHEST
    )


def outer_sum(values):
    return lax.dot_general(
        values, values, (((0,), (0,)), ((), ())), preferred_element_type=jnp.float32
    )


def blend_factor(previous, summed, fresh, damping_value, identity):
    return jnp.where(fresh == 1, 0.5 * previous + 0.5 * summed, previous) + damping_value * identity


def newton_schulz(damped, scale_value):
    block_width = damped.shape[0]
    identity = jnp.eye(block_width, dtype=jnp.float32)
    frobenius = jnp.sqrt(jnp.sum(damped * damped))
    iterate = scale_value / frobenius * identity
    for repeat in range(NS_STEPS):
        iterate = 2.0 * iterate - matrix_product(matrix_product(damped, iterate), iterate)
    return iterate.astype(jnp.bfloat16)


def apply_output_inverse(grad_low, blocks):
    block_count, block_width, unused = blocks.shape
    shaped = grad_low.reshape(grad_low.shape[0], block_count, block_width)
    product = jnp.einsum("rjb,jbc->rjc", shaped, blocks, preferred_element_type=jnp.float32)
    return product.reshape(grad_low.shape).astype(jnp.bfloat16)


def shards(
    acts_kv,
    grads_kv,
    acts_up,
    grads_up,
    prev_a_kv,
    prev_g_kv,
    prev_a_up,
    prev_g_up,
    owners,
    damping,
    init_scale,
    weights_kv,
    weights_up,
    step_size,
):
    dp_count = lax.axis_size("dp")
    dp_index = lax.axis_index("dp")
    own_index = lax.axis_index("own")
    total_tokens = acts_kv.shape[0] * dp_count
    full_kv, full_up = (
        lax.all_gather(grads_kv, "own", axis=1, tiled=True),
        lax.all_gather(grads_up, "own", axis=1, tiled=True),
    )
    column_block = acts_kv
    gradient_kv = (
        lax.psum_scatter(
            lax.dot_general(
                column_block, full_kv, (((0,), (0,)), ((), ())), preferred_element_type=jnp.float32
            ),
            "dp",
            scatter_dimension=0,
            tiled=True,
        )
        / total_tokens
    )
    column_block = acts_up
    gradient_up = (
        lax.psum_scatter(
            lax.dot_general(
                column_block, full_up, (((0,), (0,)), ((), ())), preferred_element_type=jnp.float32
            ),
            "dp",
            scatter_dimension=0,
            tiled=True,
        )
        / total_tokens
    )
    partials = (outer_sum(acts_kv), outer_sum(grads_kv), outer_sum(acts_up), outer_sum(grads_up))
    previous = (prev_a_kv[0], prev_g_kv[0], prev_a_up[0], prev_g_up[0])
    scales = lax.dynamic_index_in_dim(init_scale, own_index, 1, keepdims=False)
    summed_rows = (
        lax.psum_scatter(partials[0], "dp", scatter_dimension=0, tiled=True),
        lax.psum_scatter(partials[1], "dp", scatter_dimension=0, tiled=True),
        lax.psum_scatter(partials[2], "dp", scatter_dimension=0, tiled=True),
        lax.psum_scatter(partials[3], "dp", scatter_dimension=0, tiled=True),
    )
    summed = (
        lax.all_gather(summed_rows[0], "dp", axis=0, tiled=True),
        lax.all_gather(summed_rows[1], "dp", axis=0, tiled=True),
        lax.all_gather(summed_rows[2], "dp", axis=0, tiled=True),
        lax.all_gather(summed_rows[3], "dp", axis=0, tiled=True),
    )
    inverses = []
    for factor in range(NF):
        owner_index = owners[0, factor]
        identity = jnp.eye(previous[factor].shape[0], dtype=jnp.float32)
        damped = blend_factor(
            previous[factor],
            summed[factor] / total_tokens,
            owners[1, factor],
            damping[factor],
            identity,
        )
        local_inverse = lax.cond(
            dp_index == owner_index,
            lambda matrix: newton_schulz(matrix, scales[factor]),
            lambda matrix: jnp.zeros(matrix.shape, jnp.bfloat16),
            damped,
        )
        inverses.append(spread(local_inverse, "dp", owner_index))
    blocks_kv, blocks_up = (
        lax.all_gather(inverses[1][None], "own", axis=0, tiled=True),
        lax.all_gather(inverses[3][None], "own", axis=0, tiled=True),
    )
    low_kv = gradient_kv.astype(jnp.bfloat16)
    low_up = gradient_up.astype(jnp.bfloat16)
    right_kv = apply_output_inverse(low_kv, blocks_kv)
    right_up = apply_output_inverse(low_up, blocks_up)
    arrived = (
        lax.all_to_all(right_kv, "dp", split_axis=1, concat_axis=0, tiled=True),
        lax.all_to_all(low_kv, "dp", split_axis=1, concat_axis=0, tiled=True),
        lax.all_to_all(right_up, "dp", split_axis=1, concat_axis=0, tiled=True),
        lax.all_to_all(low_up, "dp", split_axis=1, concat_axis=0, tiled=True),
    )
    precond_kv = jnp.dot(inverses[0], arrived[0], preferred_element_type=jnp.float32)
    precond_up = jnp.dot(inverses[2], arrived[2], preferred_element_type=jnp.float32)
    term_kv = jnp.sum(precond_kv * arrived[1].astype(jnp.float32))
    term_up = jnp.sum(precond_up * arrived[3].astype(jnp.float32))
    totals = lax.psum((term_kv, term_up), ("dp", "own"))
    new_kv = weights_kv - step_size * jnp.sqrt(D * OUT_KV / totals[0]) * precond_kv
    new_up = weights_up - step_size * jnp.sqrt(D * OUT_UP / totals[1]) * precond_up
    return (new_kv, new_up)


def solution(mesh):
    return jax.shard_map(
        shards,
        mesh=mesh,
        in_specs=(
            P("dp", "own"),
            P("dp", "own"),
            P("dp", "own"),
            P("dp", "own"),
            P("own", None, None),
            P("own", None, None),
            P("own", None, None),
            P("own", None, None),
            P(),
            P(),
            P(),
            P("own", "dp"),
            P("own", "dp"),
            P(),
        ),
        out_specs=(P("own", "dp"), P("own", "dp")),
        check_vma=False,
    )
```

profile of v0, /device:TPU:0, one launch (start us, length us, event | category | flops | bytes accessed | tf_op | source)
XLA Modules:
  0.0 931.1 jit_solution(16209690147066611134)
XLA Ops:
  15.4 64.0 %reduce-scatter.7.cloned.1.call-done = f32[80,640]{1,0:T(8,128)} async-done(((f32[640,640]{1,0:T(8,128)}), f32[80,640]{1,0:T(8,128)}) %reduce-scatter.7.cloned.1.call-update) | async-done | bytes 204816 | tf_op jit(solution)/shard_map/reduce_scatter | solution.py:103
  79.5 68.1 %reduce-scatter.13.cloned.1.call-done = f32[80,640]{1,0:T(8,128)} async-done(((f32[640,640]{1,0:T(8,128)}), f32[80,640]{1,0:T(8,128)}) %reduce-scatter.13.cloned.1.call-update) | async-done | bytes 204816 | tf_op jit(solution)/shard_map/reduce_scatter | solution.py:105
  147.7 71.4 %reduce-scatter.15.cloned.1.call-done = f32[96,768]{1,0:T(8,128)} async-done(((f32[768,768]{1,0:T(8,128)}), f32[96,768]{1,0:T(8,128)}) %reduce-scatter.15.cloned.1.call-update) | async-done | bytes 294928 | tf_op jit(solution)/shard_map/reduce_scatter | solution.py:106
  223.3 59.8 %reduce-scatter.9.cloned.1.call-done = f32[32,256]{1,0:T(8,128)} async-done(((f32[256,256]{1,0:T(8,128)}), f32[32,256]{1,0:T(8,128)}) %reduce-scatter.9.cloned.1.call-update) | async-done | bytes 32784 | tf_op jit(solution)/shard_map/reduce_scatter | solution.py:104
  283.1 31.2 %all_gather.25 = f32[256,256]{1,0:T(8,128)S(1)} all-gather(f32[32,256]{1,0:T(8,128)} %reduce-scatter.9.cloned.1.call-done), channel_id=1, replica_groups=mesh['dp'=8,'own'=4] {'dp'}, dimensions={0}, use_global_device_ids=true | all-gather | bytes 294912 | tf_op jit(solution)/shard_map/all_gather | solution.py:110
  315.1 14.2 %all-gather.5.cloned.1.call-done = f32[640,640]{1,0:T(8,128)} async-done(((f32[80,640]{1,0:T(8,128)}), f32[640,640]{1,0:T(8,128)}) %all-gather.5.cloned.1.call-update) | async-done | bytes 1638416 | tf_op jit(solution)/shard_map/all_gather | solution.py:109
  332.0 29.4 %conditional.4 = (bf16[640,640]{1,0:T(8,128)(2,1)S(1)}) conditional(s32[]{:T(128)} %convert_element_type.80, () %tuple.44, (f32[4]{0:T(128)S(1)}, s32[2,4]{1,0:T(2,128)S(1)}, f32[1,640,640]{2,1,0:T(8,128)}, f32[640,640]{1,0:T(8,128)S(1)}, f32[640,640]{1,0:T(8,128)}, /*index=5*/f32[640,640]{1,0:T(8,128)}, f32[4]{0:T(128)S(1)}, ...), branch_computations={%region_1.0_spmd, %region_2.0_spmd} | conditional | flops 12590694400 | bytes 25804862 | solution.py:125
  347.9 8.2 fusion.70
  356.2 5.0 subtract_convert_fusion
  361.4 13.5 %all-gather.7.cloned.1.call-done = f32[640,640]{1,0:T(8,128)} async-done(((f32[80,640]{1,0:T(8,128)}), f32[640,640]{1,0:T(8,128)}) %all-gather.7.cloned.1.call-update) | async-done | bytes 1638416 | tf_op jit(solution)/shard_map/all_gather | solution.py:111
  374.9 9.3 conditional.6
  386.7 41.4 %all-gather.9.cloned.1.call-done = f32[768,768]{1,0:T(8,128)} async-done(((f32[96,768]{1,0:T(8,128)}), f32[768,768]{1,0:T(8,128)}) %all-gather.9.cloned.1.call-update) | async-done | bytes 2359312 | tf_op jit(solution)/shard_map/all_gather | solution.py:112
  431.3 5.4 conditional.7
  438.0 5.8 all_gather.27
  446.7 8.7 all_gather.31
  459.8 136.7 %all-reduce.4.cloned.1.call-done = (bf16[640,640]{1,0:T(8,128)(2,1)}, bf16[1,256,256]{2,1,0:T(8,128)(2,1)}, bf16[640,640]{1,0:T(8,128)(2,1)}, bf16[1,768,768]{2,1,0:T(8,128)(2,1)}) async-done(((bf16[640,640]{1,0:T(8,128)(2,1)}, bf16[1,256,256]{2,1,0:T(8,128)(2,1)}, bf16[640,640]{1,0:T(8,128)(2,1)}, bf16[1,768,768]{2,1,0:T(8,128)(2,1)}), (bf16[640,640]{1,0:T(8,128)(2,1)}, bf16[1,256,256]{2,1,0:T(8,128)(2,1)}, ...) | async-done | bytes 2949136 | tf_op jit(solution)/shard_map/psum | solution.py:15
  596.5 73.3 %reduce-scatter.11.cloned.1.call-done = f32[80,1024]{1,0:T(8,128)} async-done(((f32[640,1024]{1,0:T(8,128)}), f32[80,1024]{1,0:T(8,128)}) %reduce-scatter.11.cloned.1.call-update) | async-done | bytes 327696 | tf_op jit(solution)/shard_map/reduce_scatter | solution.py:77
  676.0 7.1 all_gather.26
  684.2 6.0 all-to-all-start
  690.2 126.9 %reduce-scatter.17.cloned.1.call-done = f32[80,3072]{1,0:T(8,128)} async-done(((f32[640,3072]{1,0:T(8,128)}), f32[80,3072]{1,0:T(8,128)}) %reduce-scatter.17.cloned.1.call-update) | async-done | bytes 983056 | tf_op jit(solution)/shard_map/reduce_scatter | solution.py:89
  822.9 32.4 %all-gather.11.cloned.1.call-done = bf16[4,768,768]{2,1,0:T(8,128)(2,1)} async-done(((bf16[1,768,768]{2,1,0:T(8,128)(2,1)}), bf16[4,768,768]{2,1,0:T(8,128)(2,1)}) %all-gather.11.cloned.1.call-update) | async-done | bytes 4718608 | tf_op jit(solution)/shard_map/all_gather | solution.py:134
  859.9 5.5 all-to-all-start.2
  867.0 12.5 %all-to-all-done.2 = bf16[80,8,384]{2,0,1:T(8,128)(2,1)S(1)} async-done(((bf16[80,8,384]{2,0,1:T(8,128)(2,1)}), bf16[80,8,384]{2,0,1:T(8,128)(2,1)S(1)}, u32[]{:S(2)}, u32[]{:S(2)}) %all-to-all-start.2) | async-done | bytes 491552 | tf_op jit(solution)/shard_map/all_to_all | solution.py:143
  882.1 38.8 %all-reduce = (f32[]{:T(128)}, f32[]{:T(128)}) all-reduce(f32[]{:T(128)} %get-tuple-element.298, f32[]{:T(128)} %get-tuple-element.300), channel_id=1, replica_groups=mesh['dp'=8,'own'=4] {'dp','own'}, use_global_device_ids=true, to_apply=%region_12.13 | all-reduce | flops 2 | bytes 16 | tf_op jit(solution)/shard_map/psum | solution.py:150
  (102 shorter events, 64.6 us)
Async XLA Ops:
  7.2 72.2 %reduce-scatter.7.cloned.1.call-start = ((), (), s32[]{:S(2)}) async-start(), calls=%async_computation.10 | async-start | bytes 1843200 | tf_op jit(solution)/shard_map/reduce_scatter | solution.py:103
  9.9 137.7 %reduce-scatter.13.cloned.1.call-start = ((), (), s32[]{:S(2)}) async-start(), calls=%async_computation.14 | async-start | bytes 1843200 | tf_op jit(solution)/shard_map/reduce_scatter | solution.py:105
  11.6 207.5 %reduce-scatter.15.cloned.1.call-start = ((), (), s32[]{:S(2)}) async-start(), calls=%async_computation.16 | async-start | bytes 2654208 | tf_op jit(solution)/shard_map/reduce_scatter | solution.py:106
  13.5 205.6 %copy-start.13 = (s32[2,4]{1,0:T(2,128)S(1)}, s32[2,4]{1,0:T(2,128)}, u32[]{:S(2)}) copy-start(s32[2,4]{1,0:T(2,128)} %param.30) | copy-start | bytes 100
  13.5 208.7 %copy-start.14 = (f32[4,4]{1,0:T(4,128)S(1)}, f32[4,4]{1,0:T(4,128)}, u32[]{:S(2)}) copy-start(f32[4,4]{1,0:T(4,128)} %param.32) | copy-start | bytes 196
  13.6 300.8 %copy-start.11 = (f32[1,256,256]{2,1,0:T(8,128)S(1)}, f32[1,256,256]{2,1,0:T(8,128)}, u32[]{:S(2)}) copy-start(f32[1,256,256]{2,1,0:T(8,128)} %param.27) | copy-start | bytes 786436
  13.6 300.8 %copy-start.15 = (f32[4]{0:T(128)S(1)}, f32[4]{0:T(128)}, u32[]{:S(2)}) copy-start(f32[4]{0:T(128)} %param.31) | copy-start | bytes 52
  13.6 269.5 %reduce-scatter.9.cloned.1.call-start = ((), (), s32[]{:S(2)}) async-start(), calls=%async_computation.12 | async-start | bytes 294912 | tf_op jit(solution)/shard_map/reduce_scatter | solution.py:104
  15.3 313.9 %all-gather.5.cloned.1.call-start = ((), (), s32[]{:S(2)}) async-start(), calls=%async_computation.11 | async-start | bytes 1843200 | tf_op jit(solution)/shard_map/all_gather | solution.py:109
  79.4 295.5 %all-gather.7.cloned.1.call-start = ((), (), s32[]{:S(2)}) async-start(), calls=%async_computation.15 | async-start | bytes 1843200 | tf_op jit(solution)/shard_map/all_gather | solution.py:111
  147.6 280.5 %all-gather.9.cloned.1.call-start = ((), (), s32[]{:S(2)}) async-start(), calls=%async_computation.17 | async-start | bytes 2654208 | tf_op jit(solution)/shard_map/all_gather | solution.py:112
  219.1 377.4 %all-reduce.4.cloned.1.call-start = ((), (), s32[]{:S(2)}) async-start(), calls=%async_computation.20 | async-start | bytes 5898240 | tf_op jit(solution)/shard_map/psum | solution.py:15
  361.4 13.5 %copy-start.1 = (bf16[640,640]{1,0:T(8,128)(2,1)}, bf16[640,640]{1,0:T(8,128)(2,1)S(1)}, u32[]{:S(2)}) copy-start(bf16[640,640]{1,0:T(8,128)(2,1)S(1)} %get-tuple-element.308) | copy-start | bytes 2457604
  438.0 231.9 %reduce-scatter.11.cloned.1.call-start = ((), (), s32[]{:S(2)}) async-start(), calls=%async_computation.13 | async-start | bytes 2949120 | tf_op jit(solution)/shard_map/reduce_scatter | solution.py:77
  445.8 371.3 %reduce-scatter.17.cloned.1.call-start = ((), (), s32[]{:S(2)}) async-start(), calls=%async_computation.19 | async-start | bytes 8847360 | tf_op jit(solution)/shard_map/reduce_scatter | solution.py:89
  459.7 395.6 %all-gather.11.cloned.1.call-start = ((), (), s32[]{:S(2)}) async-start(), calls=%async_computation.18 | async-start | bytes 5898240 | tf_op jit(solution)/shard_map/all_gather | solution.py:134
  596.5 79.5 %copy-start.12 = (bf16[1,256,256]{2,1,0:T(8,128)(2,1)S(1)}, bf16[1,256,256]{2,1,0:T(8,128)(2,1)}, u32[]{:S(2)}) copy-start(bf16[1,256,256]{2,1,0:T(8,128)(2,1)} %get-tuple-element.283) | copy-start | bytes 393220
  671.5 12.7 %all-to-all-start.1 = ((bf16[80,8,128]{2,0,1:T(8,128)(2,1)}), bf16[80,8,128]{2,0,1:T(8,128)(2,1)S(1)}, u32[]{:S(2)}, u32[]{:S(2)}) async-start(bf16[80,8,128]{2,0,1:T(8,128)(2,1)} %copy_bitcast_fusion.1), calls=%async_computation.4 | async-start | bytes 327680 | tf_op jit(solution)/shard_map/all_to_all | solution.py:142
  684.2 135.0 %all-to-all-start = ((bf16[80,8,128]{2,0,1:T(8,128)(2,1)}), bf16[80,8,128]{2,0,1:T(8,128)(2,1)S(1)}, u32[]{:S(2)}, u32[]{:S(2)}) async-start(bf16[80,8,128]{2,0,1:T(8,128)(2,1)} %copy.34), calls=%async_computation.3 | async-start | bytes 327680 | tf_op jit(solution)/shard_map/all_to_all | solution.py:141
  819.2 39.4 %copy-start.7 = (bf16[80,8,128]{2,0,1:T(8,128)(2,1)}, bf16[80,8,128]{2,0,1:T(8,128)(2,1)S(1)}, u32[]{:S(2)}) copy-start(bf16[80,8,128]{2,0,1:T(8,128)(2,1)S(1)} %all-to-all-done) | copy-start | bytes 491524
  819.2 40.6 %all-to-all-start.3 = ((bf16[80,8,384]{2,0,1:T(8,128)(2,1)}), bf16[80,8,384]{2,0,1:T(8,128)(2,1)S(1)}, u32[]{:S(2)}, u32[]{:S(2)}) async-start(bf16[80,8,384]{2,0,1:T(8,128)(2,1)} %bitcast.140), calls=%async_computation.9 | async-start | bytes 983040 | tf_op jit(solution)/shard_map/all_to_all | solution.py:144
  859.9 19.7 %all-to-all-start.2 = ((bf16[80,8,384]{2,0,1:T(8,128)(2,1)}), bf16[80,8,384]{2,0,1:T(8,128)(2,1)S(1)}, u32[]{:S(2)}, u32[]{:S(2)}) async-start(bf16[80,8,384]{2,0,1:T(8,128)(2,1)} %copy.38), calls=%async_computation.8 | async-start | bytes 983040 | tf_op jit(solution)/shard_map/all_to_all | solution.py:143
  867.0 55.3 %copy-start.5 = (f32[640,384]{1,0:T(8,128)S(1)}, f32[640,384]{1,0:T(8,128)}, u32[]{:S(2)}) copy-start(f32[640,384]{1,0:T(8,128)} %param.34) | copy-start | bytes 2949124
  882.1 41.3 %copy-start.10 = (f32[640,128]{1,0:T(8,128)S(1)}, f32[640,128]{1,0:T(8,128)}, u32[]{:S(2)}) copy-start(f32[640,128]{1,0:T(8,128)} %param.33) | copy-start | bytes 983044
  (7 other events, 26.4 us)
Sparse Core Ops, SparseCore 0:
  11.5 67.9 reduce-scatter.6
  83.2 64.3 reduce-scatter.12
  151.1 67.9 reduce-scatter.14
  222.9 60.2 reduce-scatter.8
  285.2 44.0 all-gather.4
  331.3 43.5 all-gather.6
  377.1 50.9 all-gather.8
  438.1 158.3 all-reduce.3
  600.4 69.3 reduce-scatter.10
  673.8 143.3 reduce-scatter.16
  818.8 36.5 all-gather.10
where the time goes:
time: 936 us; the launch traced here: 931 us
  waiting for transfers between devices  714 us (76%)
  blocking collectives  91.5 us (10%)
  matrix products  42.8 us (5%)
  starting transfers between devices  19.2 us (2%)
  between operations  19.1 us (2%)
  loops' own time  16.7 us (2%)
  other arithmetic  15.2 us (2%)
  local copies, waits for them, and re-layouts  12 us (1%)
    psum x1, waiting for transfers between devices, spread(): return lax.psum(jnp.where(mine, value, jnp.zeros_like(value)), axis)  137 us
    reduce_scatter x1, waiting for transfers between devices, shards(): lax.psum_scatter(lax.dot_general(column_block, full_up, (((0,), (0,)), ((...  127 us
    reduce_scatter x1, waiting for transfers between devices, shards(): lax.psum_scatter(lax.dot_general(column_block, full_kv, (((0,), (0,)), ((...  73.3 us
    reduce_scatter x1, waiting for transfers between devices, shards(): lax.psum_scatter(partials[3], 'dp', scatter_dimension=0, tiled=True)  71.4 us
    reduce_scatter x1, waiting for transfers between devices, shards(): lax.psum_scatter(partials[2], 'dp', scatter_dimension=0, tiled=True)  68.1 us
    reduce_scatter x1, waiting for transfers between devices, shards(): lax.psum_scatter(partials[0], 'dp', scatter_dimension=0, tiled=True)  64 us
    reduce_scatter x1, waiting for transfers between devices, shards(): lax.psum_scatter(partials[1], 'dp', scatter_dimension=0, tiled=True)  59.8 us
    all_gather x1, waiting for transfers between devices, shards(): lax.all_gather(summed_rows[3], 'dp', axis=0, tiled=True)  41.4 us
  transfers between devices with their start and end apart: 15, of which 12 were waited for; matrix products, arithmetic and copies ran while one was open for 6% of the time, Pallas kernels for 0%

commit v1 on v0

--- a/solution.py
+++ b/solution.py
@@ -2,6 +2,7 @@
 import jax.numpy as jnp
 from jax import lax
 from jax.sharding import PartitionSpec as P
+from jax.lax import axis_index, ppermute, psum
 
 D = 2560
 OUT_KV = 1024
@@ -129,9 +130,24 @@
             damped,
         )
         inverses.append(spread(local_inverse, "dp", owner_index))
+
+    def views_part(message, dimension_no):
+        now, r2 = (psum(1, "own"), axis_index("own"))
+        right_arr, formed = (message, 1)
+        while formed < now:
+            copies = []
+            for q in range(now):
+                copies.append((q, q ^ formed))
+            row_out = ppermute(right_arr, "own", copies)
+            v1 = jnp.concatenate([right_arr, row_out], axis=dimension_no)
+            s_next = jnp.concatenate([row_out, right_arr], axis=dimension_no)
+            right_arr = jnp.where(r2 & formed == 0, v1, s_next)
+            formed = 2 * formed
+        return right_arr
+
     blocks_kv, blocks_up = (
         lax.all_gather(inverses[1][None], "own", axis=0, tiled=True),
-        lax.all_gather(inverses[3][None], "own", axis=0, tiled=True),
+        views_part(inverses[3][None], 0),
     )
     low_kv = gradient_kv.astype(jnp.bfloat16)
     low_up = gradient_up.astype(jnp.bfloat16)

time: 936 us -> 916 us (0.979)
  waiting for transfers between devices: 714 us -> 693 us
    all_gather x1 -> x0, waiting for transfers between devices: 32.4 us -> none  [shards(): lax.all_gather(inverses[3][None], 'own', axis=0, tiled=True)]
    all_to_all x1, waiting for transfers between devices: 0.01 us -> 11.9 us  [shards(): lax.all_to_all(low_up, 'dp', split_axis=1, concat_axis=0, tiled=True)]
  transfers between devices with their start and end apart: 15 -> 16, of which waited for: 12 -> 14; matrix products, arithmetic and copies ran while one was open for 6% -> 7% of each run, Pallas kernels for 0% -> 0%
where the time goes in v1:
time: 916 us; the launch traced here: 911 us
  waiting for transfers between devices  693 us (76%)
  blocking collectives  91.5 us (10%)
  matrix products  43.7 us (5%)
  between operations  19.3 us (2%)
  other arithmetic  18 us (2%)
  loops' own time  16.8 us (2%)
  starting transfers between devices  16.5 us (2%)
  local copies, waits for them, and re-layouts  12 us (1%)
    psum x1, waiting for transfers between devices, spread(): return lax.psum(jnp.where(mine, value, jnp.zeros_like(value)), axis)  137 us
    reduce_scatter x1, waiting for transfers between devices, shards(): lax.psum_scatter(lax.dot_general(column_block, full_up, (((0,), (0,)), ((...  128 us
    reduce_scatter x1, waiting for transfers between devices, shards(): lax.psum_scatter(partials[3], 'dp', scatter_dimension=0, tiled=True)  71.4 us
    reduce_scatter x1, waiting for transfers between devices, shards(): lax.psum_scatter(partials[2], 'dp', scatter_dimension=0, tiled=True)  68.1 us
    reduce_scatter x1, waiting for transfers between devices, shards(): lax.psum_scatter(lax.dot_general(column_block, full_kv, (((0,), (0,)), ((...  65.4 us
    reduce_scatter x1, waiting for transfers between devices, shards(): lax.psum_scatter(partials[0], 'dp', scatter_dimension=0, tiled=True)  64 us
    reduce_scatter x1, waiting for transfers between devices, shards(): lax.psum_scatter(partials[1], 'dp', scatter_dimension=0, tiled=True)  59.7 us
    all_gather x1, waiting for transfers between devices, shards(): lax.all_gather(summed_rows[3], 'dp', axis=0, tiled=True)  41.5 us
  transfers between devices with their start and end apart: 16, of which 14 were waited for; matrix products, arithmetic and copies ran while one was open for 7% of the time, Pallas kernels for 0%

profile of v1, /device:TPU:0, one launch (start us, length us, event | category | flops | bytes accessed | tf_op | source)
XLA Modules:
  0.0 911.2 jit_solution(1075256479477026969)
XLA Ops:
  15.4 64.0 %reduce-scatter.7.cloned.1.call-done = f32[80,640]{1,0:T(8,128)} async-done(((f32[640,640]{1,0:T(8,128)}), f32[80,640]{1,0:T(8,128)}) %reduce-scatter.7.cloned.1.call-update) | async-done | bytes 204816 | tf_op jit(solution)/shard_map/reduce_scatter | solution.py:104
  79.5 68.1 %reduce-scatter.13.cloned.1.call-done = f32[80,640]{1,0:T(8,128)} async-done(((f32[640,640]{1,0:T(8,128)}), f32[80,640]{1,0:T(8,128)}) %reduce-scatter.13.cloned.1.call-update) | async-done | bytes 204816 | tf_op jit(solution)/shard_map/reduce_scatter | solution.py:106
  147.7 71.4 %reduce-scatter.15.cloned.1.call-done = f32[96,768]{1,0:T(8,128)} async-done(((f32[768,768]{1,0:T(8,128)}), f32[96,768]{1,0:T(8,128)}) %reduce-scatter.15.cloned.1.call-update) | async-done | bytes 294928 | tf_op jit(solution)/shard_map/reduce_scatter | solution.py:107
  223.4 59.7 %reduce-scatter.9.cloned.1.call-done = f32[32,256]{1,0:T(8,128)} async-done(((f32[256,256]{1,0:T(8,128)}), f32[32,256]{1,0:T(8,128)}) %reduce-scatter.9.cloned.1.call-update) | async-done | bytes 32784 | tf_op jit(solution)/shard_map/reduce_scatter | solution.py:105
  283.1 31.2 %all_gather.22 = f32[256,256]{1,0:T(8,128)S(1)} all-gather(f32[32,256]{1,0:T(8,128)} %reduce-scatter.9.cloned.1.call-done), channel_id=1, replica_groups=mesh['dp'=8,'own'=4] {'dp'}, dimensions={0}, use_global_device_ids=true | all-gather | bytes 294912 | tf_op jit(solution)/shard_map/all_gather | solution.py:111
  315.1 14.1 %all-gather.4.cloned.1.call-done = f32[640,640]{1,0:T(8,128)} async-done(((f32[80,640]{1,0:T(8,128)}), f32[640,640]{1,0:T(8,128)}) %all-gather.4.cloned.1.call-update) | async-done | bytes 1638416 | tf_op jit(solution)/shard_map/all_gather | solution.py:110
  332.0 29.3 %conditional.4 = (bf16[640,640]{1,0:T(8,128)(2,1)S(1)}) conditional(s32[]{:T(128)} %convert_element_type.80, () %tuple.44, (f32[4]{0:T(128)S(1)}, s32[2,4]{1,0:T(2,128)S(1)}, f32[1,640,640]{2,1,0:T(8,128)}, f32[640,640]{1,0:T(8,128)S(1)}, f32[640,640]{1,0:T(8,128)}, /*index=5*/f32[640,640]{1,0:T(8,128)}, f32[4]{0:T(128)S(1)}, ...), branch_computations={%region_1.0_spmd, %region_2.0_spmd} | conditional | flops 12590694400 | bytes 25804862 | solution.py:126
  338.2 4.6 fusion.2
  342.8 4.7 fusion.4
  347.5 8.3 fusion.79
  355.8 5.1 subtract_convert_fusion
  361.3 13.6 %all-gather.6.cloned.1.call-done = f32[640,640]{1,0:T(8,128)} async-done(((f32[80,640]{1,0:T(8,128)}), f32[640,640]{1,0:T(8,128)}) %all-gather.6.cloned.1.call-update) | async-done | bytes 1638416 | tf_op jit(solution)/shard_map/all_gather | solution.py:112
  374.9 9.1 conditional.6
  386.5 41.5 %all-gather.8.cloned.1.call-done = f32[768,768]{1,0:T(8,128)} async-done(((f32[96,768]{1,0:T(8,128)}), f32[768,768]{1,0:T(8,128)}) %all-gather.8.cloned.1.call-update) | async-done | bytes 2359312 | tf_op jit(solution)/shard_map/all_gather | solution.py:113
  431.3 5.9 conditional.7
  438.4 5.8 all_gather.24
  447.2 8.7 all_gather.27
  460.2 136.6 %all-reduce.4.cloned.1.call-done = (bf16[640,640]{1,0:T(8,128)(2,1)}, bf16[1,256,256]{2,1,0:T(8,128)(2,1)}, bf16[640,640]{1,0:T(8,128)(2,1)}, bf16[1,768,768]{2,1,0:T(8,128)(2,1)}) async-done(((bf16[640,640]{1,0:T(8,128)(2,1)}, bf16[1,256,256]{2,1,0:T(8,128)(2,1)}, bf16[640,640]{1,0:T(8,128)(2,1)}, bf16[1,768,768]{2,1,0:T(8,128)(2,1)}), (bf16[640,640]{1,0:T(8,128)(2,1)}, bf16[1,256,256]{2,1,0:T(8,128)(2,1)}, ...) | async-done | bytes 2949136 | tf_op jit(solution)/shard_map/psum | solution.py:16
  604.4 65.4 %reduce-scatter.11.cloned.1.call-done = f32[80,1024]{1,0:T(8,128)} async-done(((f32[640,1024]{1,0:T(8,128)}), f32[80,1024]{1,0:T(8,128)}) %reduce-scatter.11.cloned.1.call-update) | async-done | bytes 327696 | tf_op jit(solution)/shard_map/reduce_scatter | solution.py:78
  676.0 7.2 all_gather.23
  684.3 128.4 %reduce-scatter.17.cloned.1.call-done = f32[80,3072]{1,0:T(8,128)} async-done(((f32[640,3072]{1,0:T(8,128)}), f32[80,3072]{1,0:T(8,128)}) %reduce-scatter.17.cloned.1.call-update) | async-done | bytes 983056 | tf_op jit(solution)/shard_map/reduce_scatter | solution.py:90
  829.8 12.6 %all-to-all-done.2 = bf16[80,8,384]{2,0,1:T(8,128)(2,1)S(1)} async-done(((bf16[80,8,384]{2,0,1:T(8,128)(2,1)}), bf16[80,8,384]{2,0,1:T(8,128)(2,1)S(1)}, u32[]{:S(2)}, u32[]{:S(2)}) %all-to-all-start.2) | async-done | bytes 491552 | tf_op jit(solution)/shard_map/all_to_all | solution.py:159
  847.7 11.9 %all-to-all-done.3 = bf16[80,8,384]{2,0,1:T(8,128)(2,1)S(1)} async-done(((bf16[80,8,384]{2,0,1:T(8,128)(2,1)}), bf16[80,8,384]{2,0,1:T(8,128)(2,1)S(1)}, u32[]{:S(2)}, u32[]{:S(2)}) %all-to-all-start.3) | async-done | bytes 491552 | tf_op jit(solution)/shard_map/all_to_all | solution.py:160
  862.1 38.7 %all-reduce = (f32[]{:T(128)}, f32[]{:T(128)}) all-reduce(f32[]{:T(128)} %get-tuple-element.298, f32[]{:T(128)} %get-tuple-element.300), channel_id=1, replica_groups=mesh['dp'=8,'own'=4] {'dp','own'}, use_global_device_ids=true, to_apply=%region_12.13 | all-reduce | flops 2 | bytes 16 | tf_op jit(solution)/shard_map/psum | solution.py:166
  (100 shorter events, 73.5 us)
Async XLA Ops:
  7.2 72.2 %reduce-scatter.7.cloned.1.call-start = ((), (), s32[]{:S(2)}) async-start(), calls=%async_computation.10 | async-start | bytes 1843200 | tf_op jit(solution)/shard_map/reduce_scatter | solution.py:104
  9.9 137.7 %reduce-scatter.13.cloned.1.call-start = ((), (), s32[]{:S(2)}) async-start(), calls=%async_computation.14 | async-start | bytes 1843200 | tf_op jit(solution)/shard_map/reduce_scatter | solution.py:106
  11.6 207.5 %reduce-scatter.15.cloned.1.call-start = ((), (), s32[]{:S(2)}) async-start(), calls=%async_computation.16 | async-start | bytes 2654208 | tf_op jit(solution)/shard_map/reduce_scatter | solution.py:107
  13.6 205.6 %copy-start.11 = (s32[2,4]{1,0:T(2,128)S(1)}, s32[2,4]{1,0:T(2,128)}, u32[]{:S(2)}) copy-start(s32[2,4]{1,0:T(2,128)} %param.30) | copy-start | bytes 100
  13.6 208.7 %copy-start.12 = (f32[4,4]{1,0:T(4,128)S(1)}, f32[4,4]{1,0:T(4,128)}, u32[]{:S(2)}) copy-start(f32[4,4]{1,0:T(4,128)} %param.32) | copy-start | bytes 196
  13.6 300.7 %copy-start.9 = (f32[1,256,256]{2,1,0:T(8,128)S(1)}, f32[1,256,256]{2,1,0:T(8,128)}, u32[]{:S(2)}) copy-start(f32[1,256,256]{2,1,0:T(8,128)} %param.27) | copy-start | bytes 786436
  13.6 300.7 %copy-start.13 = (f32[4]{0:T(128)S(1)}, f32[4]{0:T(128)}, u32[]{:S(2)}) copy-start(f32[4]{0:T(128)} %param.31) | copy-start | bytes 52
  13.6 269.5 %reduce-scatter.9.cloned.1.call-start = ((), (), s32[]{:S(2)}) async-start(), calls=%async_computation.12 | async-start | bytes 294912 | tf_op jit(solution)/shard_map/reduce_scatter | solution.py:105
  15.4 313.8 %all-gather.4.cloned.1.call-start = ((), (), s32[]{:S(2)}) async-start(), calls=%async_computation.11 | async-start | bytes 1843200 | tf_op jit(solution)/shard_map/all_gather | solution.py:110
  79.4 295.5 %all-gather.6.cloned.1.call-start = ((), (), s32[]{:S(2)}) async-start(), calls=%async_computation.15 | async-start | bytes 1843200 | tf_op jit(solution)/shard_map/all_gather | solution.py:112
  147.6 280.4 %all-gather.8.cloned.1.call-start = ((), (), s32[]{:S(2)}) async-start(), calls=%async_computation.17 | async-start | bytes 2654208 | tf_op jit(solution)/shard_map/all_gather | solution.py:113
  219.1 377.6 %all-reduce.4.cloned.1.call-start = ((), (), s32[]{:S(2)}) async-start(), calls=%async_computation.19 | async-start | bytes 5898240 | tf_op jit(solution)/shard_map/psum | solution.py:16
  438.3 231.5 %reduce-scatter.11.cloned.1.call-start = ((), (), s32[]{:S(2)}) async-start(), calls=%async_computation.13 | async-start | bytes 2949120 | tf_op jit(solution)/shard_map/reduce_scatter | solution.py:78
  446.3 366.4 %reduce-scatter.17.cloned.1.call-start = ((), (), s32[]{:S(2)}) async-start(), calls=%async_computation.18 | async-start | bytes 8847360 | tf_op jit(solution)/shard_map/reduce_scatter | solution.py:90
  596.7 3.2 collective-permute-start
  596.8 79.3 %copy-start.10 = (bf16[1,256,256]{2,1,0:T(8,128)(2,1)S(1)}, bf16[1,256,256]{2,1,0:T(8,128)(2,1)}, u32[]{:S(2)}) copy-start(bf16[1,256,256]{2,1,0:T(8,128)(2,1)} %get-tuple-element.283) | copy-start | bytes 393220
  602.8 214.8 %collective-permute-start.1 = (bf16[2,768,768]{2,1,0:T(8,128)(2,1)S(1)}, bf16[2,768,768]{2,1,0:T(8,128)(2,1)}, u32[]{:S(2)}, u32[]{:S(2)}) collective-permute-start(bf16[2,768,768]{2,1,0:T(8,128)(2,1)S(1)} %maximum_select_fusion.2), channel_id=1, source_target_pairs={{0,2},{1,3},{2,0},{3,1},{4,6},{5,7},{6,4},{7,5},{8,10},{9,11},{10,... | collective-permute-start | bytes 7077896 | tf_op jit(solution)/shard_map/ppermute | solution.py:141
  671.5 142.4 %all-to-all-start.1 = ((bf16[80,8,128]{2,0,1:T(8,128)(2,1)}), bf16[80,8,128]{2,0,1:T(8,128)(2,1)S(1)}, u32[]{:S(2)}, u32[]{:S(2)}) async-start(bf16[80,8,128]{2,0,1:T(8,128)(2,1)} %copy_bitcast_fusion.1), calls=%async_computation.4 | async-start | bytes 327680 | tf_op jit(solution)/shard_map/all_to_all | solution.py:158
  813.9 11.4 %all-to-all-start = ((bf16[80,8,128]{2,0,1:T(8,128)(2,1)}), bf16[80,8,128]{2,0,1:T(8,128)(2,1)S(1)}, u32[]{:S(2)}, u32[]{:S(2)}) async-start(bf16[80,8,128]{2,0,1:T(8,128)(2,1)} %copy.34), calls=%async_computation.3 | async-start | bytes 327680 | tf_op jit(solution)/shard_map/all_to_all | solution.py:157
  822.9 23.8 %copy-start.6 = (bf16[640,640]{1,0:T(8,128)(2,1)S(1)}, bf16[640,640]{1,0:T(8,128)(2,1)}, u32[]{:S(2)}) copy-start(bf16[640,640]{1,0:T(8,128)(2,1)} %get-tuple-element.282) | copy-start | bytes 2457604
  825.3 17.1 %all-to-all-start.2 = ((bf16[80,8,384]{2,0,1:T(8,128)(2,1)}), bf16[80,8,384]{2,0,1:T(8,128)(2,1)S(1)}, u32[]{:S(2)}, u32[]{:S(2)}) async-start(bf16[80,8,384]{2,0,1:T(8,128)(2,1)} %copy.38), calls=%async_computation.8 | async-start | bytes 983040 | tf_op jit(solution)/shard_map/all_to_all | solution.py:159
  842.4 17.2 %all-to-all-start.3 = ((bf16[80,8,384]{2,0,1:T(8,128)(2,1)}), bf16[80,8,384]{2,0,1:T(8,128)(2,1)S(1)}, u32[]{:S(2)}, u32[]{:S(2)}) async-start(bf16[80,8,384]{2,0,1:T(8,128)(2,1)} %bitcast.139), calls=%async_computation.9 | async-start | bytes 983040 | tf_op jit(solution)/shard_map/all_to_all | solution.py:160
  847.7 54.6 %copy-start.5 = (f32[640,384]{1,0:T(8,128)S(1)}, f32[640,384]{1,0:T(8,128)}, u32[]{:S(2)}) copy-start(f32[640,384]{1,0:T(8,128)} %param.34) | copy-start | bytes 2949124
  862.1 41.2 %copy-start.8 = (f32[640,128]{1,0:T(8,128)S(1)}, f32[640,128]{1,0:T(8,128)}, u32[]{:S(2)}) copy-start(f32[640,128]{1,0:T(8,128)} %param.33) | copy-start | bytes 983044
  (6 other events, 25.8 us)
Sparse Core Ops, SparseCore 0:
  11.5 67.9 reduce-scatter.6
  83.2 64.3 reduce-scatter.12
  151.1 67.9 reduce-scatter.14
  222.9 60.2 reduce-scatter.8
  285.2 44.0 all-gather.3
  331.3 43.6 all-gather.5
  377.1 50.9 all-gather.7
  438.4 158.2 all-reduce.3
  600.7 69.1 reduce-scatter.10
  673.8 138.8 reduce-scatter.16
